TPU v7x, 32 devices: a whole 2x2x4 slice. The times are simulated.
32 devices in a mesh: group: 4 (over x, core), tensor: 8 (over z, y).
Axes of the slice: x: 2, y: 2, z: 4, core: 2. Of those that a mesh axis runs over, the one named last changes fastest.
Arguments:
- hidden: bfloat16 [512, 8192], P('group'), may hold values from -6 to 6
- norm_gain: bfloat16 [8192], replicated, may hold values from 0.5 to 1.5
- query_matrix: bfloat16 [8192, 8192], P(None, 'tensor'), may hold values from -0.0625 to 0.0625
- output_weight: bfloat16 [8192, 8192], P('tensor'), may hold values from -0.0625 to 0.0625
- kv_pages: bfloat16 [768, 8, 32, 256], P('group', 'tensor'), may hold values from -400 to 400
- page_order: int32 [4, 192], P('group'), may hold values from 0 to 191, each once within a row
- page_counts: int32 [4, 128], P('group'), may hold values from 1 to 8, 192 in all within a row
- page_trims: int32 [4, 128], P('group'), may hold values from 0 to 31
- adapter_store: bfloat16 [32, 8192, 256], P('group', 'tensor'), may hold values from -0.0625 to 0.0625
- store_route: int32 [32, 1], replicated, may hold values from 0 to 3; in each aligned block of 8 rows (0 to 7, 8 to 15, ...) at most 4 rows name the same one
- store_slot: int32 [32], replicated, may hold values from 0 to 7
Outputs:
- layer_out: bfloat16 [512, 8192], P('group')
Inputs may be any that keep to these rules, and one draw needn't show every extreme that they name: `store_route`: in each group's block of 8 segments no store group is named more than 4 times. `page_order`: each group's row names each of its 192 pages once. `page_counts`: each group's counts sum to 192.
All inputs are finite; a program needn't handle non-finite values.
Results may differ from a plain program's by a relative error of at most 0.0092.
Values may be sent and summed in bfloat16 or wider, within the bound.
No kernel may reach another device: no remote copies, remote signals or barrier semaphores. Data moves between devices by JAX's collectives and lax.ppermute only.
A program may use at most 128 MiB of HBM per device.

v0:
```python
import math
import jax
import jax.numpy as jnp
from jax import lax
from jax.sharding import PartitionSpec as P

KVH = 8
HD = 128
SEG = 16
PAGES_MAX = 8
adapter_scale = 2.0
norm_eps = 1e-05
rope_base = 500000.0


def partner_2(value, axis, stride):
    return lax.ppermute(value, axis, [(i, i ^ 1 << stride) for i in range(lax.axis_size(axis))])


def rotate(queries, positions):
    half_dim = queries.shape[-1] // 2
    frequency = rope_base ** (-(jnp.arange(half_dim).astype(jnp.float32) * 2.0) / queries.shape[-1])
    angles = positions[:, None] * frequency[None, :]
    cosine = jnp.cos(angles)[:, None, :]
    sine_table = jnp.sin(angles)[:, None, :]
    lower_part = queries[..., :half_dim]
    upper_part = queries[..., half_dim:]
    return jnp.concatenate(
        [
            lower_part * cosine - upper_part * sine_table,
            upper_part * cosine + lower_part * sine_table,
        ],
        axis=-1,
    )


def rank_total(partial_value):
    return lax.psum(partial_value, "tensor")


def body(
    hidden,
    norm_gain,
    query_matrix,
    output_weight,
    kv_pages,
    page_order,
    page_counts,
    page_trims,
    adapter_store,
    store_route,
    store_slot,
):
    tensor_size = lax.axis_size("tensor")
    group_size = lax.axis_size("group")
    shard_tensor_index = lax.axis_index("tensor")
    group_index = lax.axis_index("group")
    row_count = hidden.shape[0]
    local_width = query_matrix.shape[1]
    heads_dev = local_width // HD
    split_count = tensor_size // KVH
    part_index = shard_tensor_index % split_count
    pool_size = kv_pages.shape[0]
    half_size = kv_pages.shape[2]
    stored = adapter_store.shape[0]
    lane_count = adapter_store.shape[2]
    adapter_rank_width = lane_count // 4
    seg_count = row_count // SEG
    capacity = max(2, (2 * seg_count + group_size - 1) // group_size)
    hidden_float32 = hidden.astype(jnp.float32)
    inv_rms = lax.rsqrt(jnp.mean(hidden_float32 * hidden_float32, axis=1, keepdims=True) + norm_eps)
    normalized_hidden = (hidden_float32 * inv_rms * norm_gain.astype(jnp.float32)[None, :]).astype(
        jnp.bfloat16
    )
    normalized_local = lax.dynamic_slice_in_dim(
        normalized_hidden, shard_tensor_index * local_width, local_width, 1
    )
    route_table = store_route[:, 0].reshape(group_size, seg_count)
    slot_table = store_slot.reshape(group_size, seg_count)
    earlier = jnp.arange(seg_count)[:, None] > jnp.arange(seg_count)[None, :]
    same_route = route_table[:, :, None] == route_table[:, None, :]
    slot_rank = jnp.sum(jnp.where(same_route & earlier[None, :, :], 1, 0), axis=2).astype(jnp.int32)
    target = route_table * capacity + slot_rank
    own_target = lax.dynamic_index_in_dim(target, group_index, 0, keepdims=False)
    placing = (jnp.arange(group_size * capacity)[:, None] == own_target[None, :]).astype(
        jnp.bfloat16
    )
    wanted = (route_table == group_index)[:, :, None] & (
        slot_rank[:, :, None] == jnp.arange(capacity)[None, None, :]
    )
    slot_hot = slot_table[:, :, None] == jnp.arange(stored)[None, None, :]
    choosing = (
        jnp.einsum("gkc,gka->gca", wanted.astype(jnp.float32), slot_hot.astype(jnp.float32))
        .reshape(group_size * capacity, stored)
        .astype(jnp.bfloat16)
    )
    store_flat = adapter_store.reshape(stored, local_width * lane_count)
    outgoing = jnp.dot(choosing, store_flat, preferred_element_type=jnp.float32).astype(
        jnp.bfloat16
    )
    chosen = outgoing.reshape(group_size * capacity, local_width, lane_count)

    def apply_adapter_update(input_rows, leading_column, trailing_column):
        sending = jnp.dot(
            placing,
            input_rows.reshape(seg_count, SEG * local_width),
            preferred_element_type=jnp.float32,
        ).astype(jnp.bfloat16)
        received = lax.all_to_all(
            sending.reshape(group_size, capacity * SEG, local_width),
            "group",
            split_axis=0,
            concat_axis=0,
            tiled=True,
        )
        received = received.reshape(group_size * capacity, SEG, local_width)
        partial_value = jnp.einsum(
            "nsd,ndr->nsr",
            received,
            chosen[:, :, leading_column : leading_column + adapter_rank_width],
            preferred_element_type=jnp.float32,
        )
        low_rank = rank_total(partial_value).astype(jnp.bfloat16)
        result = jnp.einsum(
            "nsr,ndr->nsd",
            low_rank,
            chosen[:, :, trailing_column : trailing_column + adapter_rank_width],
            preferred_element_type=jnp.float32,
        )
        returned = lax.all_to_all(
            result.reshape(group_size, capacity * SEG, local_width),
            "group",
            split_axis=0,
            concat_axis=0,
            tiled=True,
        )
        returned = returned.reshape(group_size * capacity, SEG * local_width)
        gathered = jnp.dot(
            placing.T.astype(jnp.float32),
            returned,
            precision=lax.Precision.HIGHEST,
            preferred_element_type=jnp.float32,
        )
        return gathered.reshape(row_count, local_width)

    lengths = page_counts[0] * split_count * half_size - page_trims[0]
    query_float32 = jnp.dot(
        normalized_hidden, query_matrix, preferred_element_type=jnp.float32
    ) + adapter_scale * apply_adapter_update(normalized_local, 0, 2 * adapter_rank_width)
    queries = rotate(
        query_float32.reshape(row_count, heads_dev, HD), (lengths - 1).astype(jnp.float32)
    ).astype(jnp.bfloat16)
    for level_bit in range(split_count.bit_length() - 1):
        partner = partner_2(queries, "tensor", level_bit)
        upper_bit = shard_tensor_index // 2**level_bit % 2
        queries = jnp.where(
            upper_bit == 0,
            jnp.concatenate([queries, partner], axis=1),
            jnp.concatenate([partner, queries], axis=1),
        )
    offsets = jnp.cumsum(page_counts[0]) - page_counts[0]
    page_slot = jnp.clip(
        offsets[:, None] + jnp.arange(PAGES_MAX, dtype=jnp.int32)[None, :], 0, pool_size - 1
    )
    page_ids = page_order[0][page_slot]
    cached = kv_pages[:, 0][page_ids].reshape(row_count, PAGES_MAX * half_size, 2 * HD)
    positions = (
        jnp.arange(PAGES_MAX, dtype=jnp.int32)[:, None] * (split_count * half_size)
        + part_index * half_size
        + jnp.arange(half_size, dtype=jnp.int32)[None, :]
    ).reshape(-1)
    usable = positions[None, :] < lengths[:, None]
    scores = jnp.einsum(
        "rgd,rpd->rgp", queries, cached[..., :HD], preferred_element_type=jnp.float32
    ) / math.sqrt(HD)
    masked = jnp.where(usable[:, None, :], scores, -1e30)
    row_max = jnp.max(masked, axis=2)
    weights = jnp.where(usable[:, None, :], jnp.exp(masked - row_max[..., None]), 0.0).astype(
        jnp.bfloat16
    )
    totals = jnp.sum(weights.astype(jnp.float32), axis=2)
    output_part = jnp.einsum(
        "rgp,rpd->rgd", weights, cached[..., HD:], preferred_element_type=jnp.float32
    )
    for level_bit in range(split_count.bit_length() - 1):
        other_out, other_max, other_total = partner_2(
            (output_part, row_max, totals), "tensor", level_bit
        )
        joint_max = jnp.maximum(row_max, other_max)
        own_scale = jnp.exp(row_max - joint_max)
        other_scale = jnp.exp(other_max - joint_max)
        output_part = output_part * own_scale[..., None] + other_out * other_scale[..., None]
        totals = totals * own_scale + other_total * other_scale
        row_max = joint_max
    attended_all = output_part / totals[..., None]
    attention_result = (
        lax.dynamic_slice_in_dim(attended_all, part_index * heads_dev, heads_dev, 1)
        .reshape(row_count, local_width)
        .astype(jnp.bfloat16)
    )
    partial_output = jnp.dot(attention_result, output_weight, preferred_element_type=jnp.float32)
    adapter_output = adapter_scale * apply_adapter_update(
        attention_result, adapter_rank_width, 3 * adapter_rank_width
    )
    own_cols = (
        lax.dynamic_slice_in_dim(partial_output, shard_tensor_index * local_width, local_width, 1)
        + adapter_output
    )
    partial_output = lax.dynamic_update_slice_in_dim(
        partial_output, own_cols, shard_tensor_index * local_width, 1
    )
    summed = lax.psum(partial_output, "tensor")
    layer_out = (hidden_float32 + summed).astype(jnp.bfloat16)
    return layer_out


def solution(mesh):
    in_specs = (
        P("group", None),
        P(),
        P(None, "tensor"),
        P("tensor", None),
        P("group", "tensor", None, None),
        P("group", None),
        P("group", None),
        P("group", None),
        P("group", "tensor", None),
        P(),
        P(),
    )
    out_specs = P("group", None)
    return jax.shard_map(body, mesh=mesh, in_specs=in_specs, out_specs=out_specs, check_vma=False)
```

profile of v0, /device:TPU:0, one launch (start us, length us, event | category | flops | bytes accessed | tf_op | source)
XLA Modules:
  0.0 380.9 jit_solution(1167026221294067381)
XLA Ops:
  6.5 2.2 fusion.5
  8.8 0.5 broadcast.207
  9.3 1.3 reduce.4
  10.7 0.2 select_reduce_fusion
  11.0 0.7 convert_element_type.70
  11.7 2.2 fusion.7
  13.9 1.3 copy-done.3
  15.2 0.8 reshape.284
  16.1 2.0 convolution_convert_fusion.2
  18.1 2.1 reshape.285
  20.2 4.2 %all-to-all-start = ((bf16[4,64,1024]{2,1,0:T(8,128)(2,1)}), bf16[4,64,1024]{2,1,0:T(8,128)(2,1)}, u32[]{:S(2)}, u32[]{:S(2)}) async-start(bf16[4,64,1024]{2,1,0:T(8,128)(2,1)} %reshape.285), calls=%async_computation | async-start | bytes 1048576 | tf_op jit(solution)/shard_map/all_to_all | solution.py:109
  24.7 0.1 copy.20
  24.8 0.2 reduce-window.8
  25.3 6.8 %gather_fusion = s32[1024]{0:T(1024)S(1)} fusion(s32[192]{0:T(256)S(1)} %bitcast.51, s32[1024]{0:T(1024)S(1)} %broadcast_clamp_fusion), kind=kCustom, calls=%fused_computation | custom fusion | bytes 12288 | tf_op jit(solution)/shard_map/gather | solution.py:165
  32.4 4.6 %copy.27 = bf16[1,8,1024,256]{3,1,2,0:T(8,128)(2,1)S(1)} copy(bf16[1,8,1024,256]{3,2,1,0:T(8,128)(2,1)} %bitcast.61) | data formatting | bytes 8388608
  36.9 0.2 convolution_convert_fusion.3
  37.1 5.5 %convolution_convert_fusion = bf16[16,262144]{1,0:T(8,128)(2,1)} fusion(bf16[16,8]{1,0:T(8,128)(2,1)S(1)} %bitcast.65, bf16[8,262144]{1,0:T(8,128)(2,1)S(1)} %bitcast.59), kind=kOutput, calls=%fused_computation.3 | convolution fusion | flops 71303168 | bytes 12583168 | tf_op jit(solution)/shard_map/dot_general | solution.py:98
  42.7 8.5 %copy.28 = bf16[2,8,1024,256]{3,2,1,0:T(8,128)(2,1)} copy(bf16[2,8,1024,256]{3,1,2,0:T(8,128)(2,1)} %bitcast.56) | data formatting | bytes 16777216
  51.1 3.0 fusion.15
  54.2 40.2 %psum.21 = bf16[16,16,64]{2,1,0:T(8,128)(2,1)S(1)} all-reduce(f32[16,16,64]{2,1,0:T(8,128)S(1)} %fusion.15), channel_id=1, replica_groups=mesh['group'=4,'tensor'=8] {'tensor'}, use_global_device_ids=true, to_apply=%region_2.3 | all-reduce | flops 16384 | bytes 98304 | tf_op jit(solution)/shard_map/psum | solution.py:38
  94.4 4.4 %fusion.13 = f32[16,16,1024]{2,1,0:T(8,128)} fusion(bf16[16,1024,256]{2,1,0:T(8,128)(2,1)} %bitcast.53, bf16[16,16,64]{2,1,0:T(8,128)(2,1)S(1)} %psum.21), kind=kOutput, calls=%fused_computation.23 | convolution fusion | flops 33554432 | bytes 5275648 | tf_op jit(solution)/shard_map/nsr,ndr->nsd/dot_general | solution.py:124
  98.7 4.4 %all-to-all-start.1 = ((f32[4,64,1024]{2,1,0:T(8,128)}), f32[4,64,1024]{2,1,0:T(8,128)}, u32[]{:S(2)}, u32[]{:S(2)}) async-start(f32[4,64,1024]{2,1,0:T(8,128)} %bitcast.62), calls=%async_computation.1 | async-start | bytes 2097152 | tf_op jit(solution)/shard_map/all_to_all | solution.py:130
  103.2 12.4 %gather_fusion.1 = bf16[1024,32,256]{2,1,0:T(8,128)(2,1)} fusion(bf16[192,32,256]{2,1,0:T(8,128)(2,1)S(1)} %bitcast.50, s32[1024]{0:T(1024)S(1)} %broadcast_clamp_fusion.1), kind=kCustom, calls=%fused_computation.1 | custom fusion | bytes 33558528 | tf_op jit(solution)/shard_map/gather | solution.py:166
  115.7 0.3 multiply_cosine_fusion
  116.0 1.4 all-to-all-done.1
  117.5 1.4 reshape.290
  118.9 1.4 convolution_multiply_fusion.1
  120.2 1.1 mul.135
  121.4 8.1 %fusion.27 = f32[16,8,8,128]{3,1,2,0:T(8,128)S(1)} fusion(f32[128,1024]{1,0:T(8,128)S(1)} %mul.135, bf16[128,8192]{1,0:T(8,128)(2,1)S(1)} %copy-done.4, bf16[8192,1024]{1,0:T(8,128)(2,1)} %param.13), kind=kOutput, calls=%fused_computation.34 | convolution fusion | flops 2147614720 | bytes 19922944 | tf_op jit(solution)/shard_map/dot_general | solution.py:147
  129.6 0.3 subtract_convert_fusion
  129.9 5.9 %convert_reduce_fusion = (f32[128,8]{1,0:T(8,128)S(1)}, bf16[128,8,256]{2,1,0:T(8,128)(2,1)S(1)}) fusion(pred[128,256]{1,0:T(8,128)(4,1)S(1)} %broadcast_compare_fusion, bf16[128,256,256]{2,1,0:T(8,128)(2,1)} %bitcast.57, bf16[128,8,64]{2,1,0:T(8,128)(2,1)S(1)} %get-tuple-element.8, bf16[128,8,64]{2,1,0:T(8,128)(2,1)S(1)} %get-tuple-element.7), kind=kOutput, calls=%fused_computation.36 | convolution fusion | flops 69468416 | bytes 9506816 | tf_op jit(solution)/shard_map/sub | solution.py:178
  135.8 4.6 %fusion.31 = bf16[128,8,128]{2,1,0:T(8,128)(2,1)S(1)} fusion(bf16[128,8,256]{2,1,0:T(8,128)(2,1)S(1)} %get-tuple-element.13, bf16[128,256,256]{2,1,0:T(8,128)(2,1)} %bitcast.58, f32[128,8]{1,0:T(8,128)S(1)} %get-tuple-element.12), kind=kOutput, calls=%fused_computation.38 | convolution fusion | flops 67371008 | bytes 9179136 | tf_op jit(solution)/shard_map/rgp,rpd->rgd/dot_general | solution.py:182
  140.3 0.1 convert_element_type.83
  140.5 0.3 convolution_convert_fusion.1
  140.7 0.2 reshape.295
  141.0 11.2 %all_to_all.20 = bf16[4,64,1024]{2,1,0:T(8,128)(2,1)S(1)} all-to-all(bf16[4,64,1024]{2,1,0:T(8,128)(2,1)S(1)} %reshape.295), channel_id=1, replica_groups=mesh['group'=4,'tensor'=8] {'group'}, dimensions={0} | all-to-all | bytes 1048576 | tf_op jit(solution)/shard_map/all_to_all | solution.py:109
  152.2 3.5 fusion.11
  155.7 34.2 %psum.22 = bf16[16,16,64]{2,1,0:T(8,128)(2,1)S(1)} all-reduce(f32[16,16,64]{2,1,0:T(8,128)S(1)} %fusion.11), channel_id=1, replica_groups=mesh['group'=4,'tensor'=8] {'tensor'}, use_global_device_ids=true, to_apply=%region_6.7 | all-reduce | flops 16384 | bytes 98304 | tf_op jit(solution)/shard_map/psum | solution.py:38
  189.9 4.5 %fusion.9 = f32[16,16,1024]{2,1,0:T(8,128)} fusion(bf16[16,1024,256]{2,1,0:T(8,128)(2,1)} %bitcast.55, bf16[16,16,64]{2,1,0:T(8,128)(2,1)S(1)} %psum.22), kind=kOutput, calls=%fused_computation.19 | convolution fusion | flops 33554432 | bytes 5275648 | tf_op jit(solution)/shard_map/nsr,ndr->nsd/dot_general | solution.py:124
  194.3 3.5 all-to-all-start.3
  197.9 0.3 all-reduce.2.cloned.1.call-start
  198.1 10.1 %fusion.34 = f32[128,8192]{1,0:T(8,128)} fusion(bf16[1024,8192]{1,0:T(8,128)(2,1)} %param.14, bf16[16,8,8,128]{3,2,1,0:T(8,128)(2,1)S(1)} %bitcast.64), kind=kOutput, calls=%fused_computation.42 | convolution fusion | flops 2147483648 | bytes 21233664 | tf_op jit(solution)/shard_map/dot_general | solution.py:201
  208.2 4.0 %all-to-all-done.3 = f32[4,64,1024]{2,1,0:T(8,128)S(1)} async-done(((f32[4,64,1024]{2,1,0:T(8,128)}), f32[4,64,1024]{2,1,0:T(8,128)S(1)}, u32[]{:S(2)}, u32[]{:S(2)}) %all-to-all-start.3) | async-done | bytes 1048608 | tf_op jit(solution)/shard_map/all_to_all | solution.py:130
  212.3 0.2 reshape.298
  212.5 0.5 convolution_multiply_fusion
  213.1 1.9 add_dynamic-update-slice_fusion
  215.0 154.5 %all-reduce.2.cloned.1.call-done = f32[128,8192]{1,0:T(8,128)} async-done(((f32[128,8192]{1,0:T(8,128)}), f32[128,8192]{1,0:T(8,128)}) %all-reduce.2.cloned.1.call-update) | async-done | bytes 4194320 | tf_op jit(solution)/shard_map/psum | solution.py:212
  369.5 4.6 %fusion.8 = bf16[128,8192]{1,0:T(8,128)(2,1)} fusion(f32[128,8192]{1,0:T(8,128)} %all-reduce.2.cloned.1.call-done, bf16[128,8192]{1,0:T(8,128)(2,1)} %param.11), kind=kLoop, calls=%fused_computation.18 | loop fusion | flops 3145728 | bytes 8388608 | tf_op jit(solution)/shard_map/convert_element_type | solution.py:213
  (41 shorter events, 1.2 us)
Async XLA Ops:
  6.5 96.6 %copy-start = (bf16[192,1,32,256]{3,2,1,0:T(8,128)(2,1)S(1)}, bf16[192,1,32,256]{3,2,1,0:T(8,128)(2,1)}, u32[]{:S(2)}) copy-start(bf16[192,1,32,256]{3,2,1,0:T(8,128)(2,1)} %param.15) | copy-start | bytes 9437188
  8.8 15.7 %copy-start.6 = (s32[32]{0:T(128)S(1)}, s32[32]{0:T(128)}, u32[]{:S(2)}) copy-start(s32[32]{0:T(128)} %param.21) | copy-start | bytes 388
  8.8 15.9 %copy-start.5 = (s32[1,128]{1,0:T(1,128)S(1)}, s32[1,128]{1,0:T(1,128)}, u32[]{:S(2)}) copy-start(s32[1,128]{1,0:T(1,128)} %param.17) | copy-start | bytes 1540
  11.7 13.4 %copy-start.7 = (s32[1,128]{1,0:T(1,128)S(1)}, s32[1,128]{1,0:T(1,128)}, u32[]{:S(2)}) copy-start(s32[1,128]{1,0:T(1,128)} %param.18) | copy-start | bytes 1540
  11.7 13.6 %copy-start.2 = (s32[1,192]{1,0:T(1,128)S(1)}, s32[1,192]{1,0:T(1,128)}, u32[]{:S(2)}) copy-start(s32[1,192]{1,0:T(1,128)} %param.16) | copy-start | bytes 2308
  13.9 1.3 copy-start.3
  20.2 30.9 %all-to-all-start = ((bf16[4,64,1024]{2,1,0:T(8,128)(2,1)}), bf16[4,64,1024]{2,1,0:T(8,128)(2,1)}, u32[]{:S(2)}, u32[]{:S(2)}) async-start(bf16[4,64,1024]{2,1,0:T(8,128)(2,1)} %reshape.285), calls=%async_computation | async-start | bytes 1048576 | tf_op jit(solution)/shard_map/all_to_all | solution.py:109
  98.7 18.7 %all-to-all-start.1 = ((f32[4,64,1024]{2,1,0:T(8,128)}), f32[4,64,1024]{2,1,0:T(8,128)}, u32[]{:S(2)}, u32[]{:S(2)}) async-start(f32[4,64,1024]{2,1,0:T(8,128)} %bitcast.62), calls=%async_computation.1 | async-start | bytes 2097152 | tf_op jit(solution)/shard_map/all_to_all | solution.py:130
  115.6 5.8 %copy-start.4 = (bf16[128,8192]{1,0:T(8,128)(2,1)S(1)}, bf16[128,8192]{1,0:T(8,128)(2,1)}, u32[]{:S(2)}) copy-start(bf16[128,8192]{1,0:T(8,128)(2,1)} %copy-done.3) | copy-start | bytes 6291460
  194.3 17.9 %all-to-all-start.3 = ((f32[4,64,1024]{2,1,0:T(8,128)}), f32[4,64,1024]{2,1,0:T(8,128)S(1)}, u32[]{:S(2)}, u32[]{:S(2)}) async-start(f32[4,64,1024]{2,1,0:T(8,128)} %bitcast.11), calls=%async_computation.3 | async-start | bytes 2097152 | tf_op jit(solution)/shard_map/all_to_all | solution.py:130
  197.9 171.6 %all-reduce.2.cloned.1.call-start = ((), (), s32[]{:S(2)}) async-start(), calls=%async_computation.4 | async-start | bytes 8388608 | tf_op jit(solution)/shard_map/psum | solution.py:212
  215.0 159.1 %copy-start.1 = (bf16[192,1,32,256]{3,2,1,0:T(8,128)(2,1)S(1)}, bf16[192,1,32,256]{3,2,1,0:T(8,128)(2,1)}, u32[]{:S(2)}) copy-start(bf16[192,1,32,256]{3,2,1,0:T(8,128)(2,1)} %param.15) | copy-start | bytes 9437188
Sparse Core Ops, SparseCore 0:
  215.1 154.3 all-reduce.1
where the time goes:
time: 382 us; the launch traced here: 381 us
  waiting for transfers between devices  160 us (42%)
  blocking collectives  85.6 us (22%)
  matrix products  53.8 us (14%)
  local copies, waits for them, and re-layouts  41.1 us (11%)
  other arithmetic  14.4 us (4%)
  between operations  13.7 us (4%)
  starting transfers between devices  12.4 us (3%)
    psum x1, waiting for transfers between devices, body(): summed = lax.psum(partial_output, 'tensor')  154 us
    psum x2, blocking collectives, rank_total(): return lax.psum(partial_value, 'tensor')  74.4 us
    unnamed x20, local copies, waits for them, and re-layouts  15 us
    gather x1, local copies, waits for them, and re-layouts, body(): kv_pages[:, 0][page_ids].reshape(row_count, PAGES_MAX * half_size, 2 * HD)  12.4 us
    all_to_all x1, blocking collectives, apply_adapter_update(): lax.all_to_all(sending.reshape(group_size, capacity * SEG, local_width),...  11.2 us
    dot_general x1, matrix products, body(): jnp.dot(attention_result, output_weight, preferred_element_type=jnp.float32)  10.1 us
    dot_general x2, matrix products, apply_adapter_update(): jnp.einsum('nsr,ndr->nsd', low_rank, chosen[:, :, trailing_column:trailin...  8.83 us
    dot_general x1, matrix products, body(): jnp.dot(normalized_hidden, query_matrix, preferred_element_type=jnp.float32)  8.1 us
  transfers between devices with their start and end apart: 4, of which 3 were waited for; matrix products, arithmetic and copies ran while one was open for 13% of the time, Pallas kernels for 0%

commit v1 on v0

--- a/solution.py
+++ b/solution.py
@@ -11,6 +11,14 @@
 adapter_scale = 2.0
 norm_eps = 1e-05
 rope_base = 500000.0
+
+
+def sheet_define(inputs):
+    k_all = lax.axis_size("tensor")
+    out_arr = inputs
+    for d in [[(c, c ^ k) for c in range(k_all)] for k in (1, 2, 4, 8, 16) if k < k_all]:
+        out_arr = out_arr + lax.ppermute(out_arr, "tensor", d)
+    return out_arr
 
 
 def partner_2(value, axis, stride):
@@ -209,7 +217,7 @@
     partial_output = lax.dynamic_update_slice_in_dim(
         partial_output, own_cols, shard_tensor_index * local_width, 1
     )
-    summed = lax.psum(partial_output, "tensor")
+    summed = sheet_define(partial_output)
     layer_out = (hidden_float32 + summed).astype(jnp.bfloat16)
     return layer_out
 

time: 382 us -> 579 us (1.52)
  waiting for transfers between devices: 160 us -> 370 us
  between operations: 13.7 us -> 0.33 us
    ppermute x0 -> x3, waiting for transfers between devices: none -> 364 us  [sheet_define(): out_arr = out_arr + lax.ppermute(out_arr, 'tensor', d)]
    psum x1 -> x0, waiting for transfers between devices: 154 us -> none  [body(): summed = lax.psum(partial_output, 'tensor')]
    unnamed x20 -> x22, local copies, waits for them, and re-layouts: 15 us -> 15 us
  transfers between devices with their start and end apart: 4 -> 6, of which waited for: 3 -> 5; matrix products, arithmetic and copies ran while one was open for 13% -> 9% of each run, Pallas kernels for 0% -> 0%
where the time goes in v1:
time: 579 us; the launch traced here: 578 us
  waiting for transfers between devices  370 us (64%)
  blocking collectives  85.6 us (15%)
  matrix products  53.8 us (9%)
  local copies, waits for them, and re-layouts  41.1 us (7%)
  other arithmetic  15 us (3%)
  starting transfers between devices  12.7 us (2%)
    ppermute x3, waiting for transfers between devices, sheet_define(): out_arr = out_arr + lax.ppermute(out_arr, 'tensor', d)  364 us
    psum x2, blocking collectives, rank_total(): return lax.psum(partial_value, 'tensor')  74.4 us
    unnamed x22, local copies, waits for them, and re-layouts  15 us
    gather x1, local copies, waits for them, and re-layouts, body(): kv_pages[:, 0][page_ids].reshape(row_count, PAGES_MAX * half_size, 2 * HD)  12.4 us
  transfers between devices with their start and end apart: 6, of which 5 were waited for; matrix products, arithmetic and copies ran while one was open for 9% of the time, Pallas kernels for 0%

profile of v1, /device:TPU:0, one launch (start us, length us, event | category | flops | bytes accessed | tf_op | source)
XLA Modules:
  0.0 578.3 jit_solution(12545940444229090303)
XLA Ops:
  0.0 2.2 fusion.5
  2.3 0.5 broadcast.207
  2.8 1.3 reduce.4
  4.2 0.2 select_reduce_fusion
  4.4 0.7 convert_element_type.70
  5.1 2.2 fusion.7
  7.4 1.3 copy-done.4
  8.7 0.8 reshape.284
  9.5 2.0 convolution_convert_fusion.2
  11.5 2.1 reshape.285
  13.7 4.2 all-to-all-start
  18.8 6.8 %gather_fusion = s32[1024]{0:T(1024)S(1)} fusion(s32[192]{0:T(256)S(1)} %bitcast.51, s32[1024]{0:T(1024)S(1)} %broadcast_clamp_fusion), kind=kCustom, calls=%fused_computation | custom fusion | bytes 12288 | tf_op jit(solution)/shard_map/gather | solution.py:173
  25.8 4.6 copy.27
  30.4 0.2 convolution_convert_fusion.3
  30.6 5.5 convolution_convert_fusion
  36.1 8.5 %copy.28 = bf16[2,8,1024,256]{3,2,1,0:T(8,128)(2,1)} copy(bf16[2,8,1024,256]{3,1,2,0:T(8,128)(2,1)} %bitcast.56) | data formatting | bytes 16777216
  44.6 3.0 fusion.15
  47.6 40.2 %psum.14 = bf16[16,16,64]{2,1,0:T(8,128)(2,1)S(1)} all-reduce(f32[16,16,64]{2,1,0:T(8,128)S(1)} %fusion.15), channel_id=1, replica_groups=mesh['group'=4,'tensor'=8] {'tensor'}, use_global_device_ids=true, to_apply=%region_2.3 | all-reduce | flops 16384 | bytes 98304 | tf_op jit(solution)/shard_map/psum | solution.py:46
  87.8 4.4 fusion.13
  92.2 4.4 all-to-all-start.1
  96.7 12.4 %gather_fusion.1 = bf16[1024,32,256]{2,1,0:T(8,128)(2,1)} fusion(bf16[192,32,256]{2,1,0:T(8,128)(2,1)S(1)} %bitcast.50, s32[1024]{0:T(1024)S(1)} %broadcast_clamp_fusion.1), kind=kCustom, calls=%fused_computation.1 | custom fusion | bytes 33558528 | tf_op jit(solution)/shard_map/gather | solution.py:174
  109.2 0.3 multiply_cosine_fusion
  109.5 1.4 all-to-all-done.1
  110.9 1.4 reshape.290
  112.4 1.4 convolution_multiply_fusion.1
  113.7 1.1 mul.135
  114.9 8.1 %fusion.27 = f32[16,8,8,128]{3,1,2,0:T(8,128)S(1)} fusion(f32[128,1024]{1,0:T(8,128)S(1)} %mul.135, bf16[128,8192]{1,0:T(8,128)(2,1)S(1)} %copy-done.5, bf16[8192,1024]{1,0:T(8,128)(2,1)} %param.13), kind=kOutput, calls=%fused_computation.34 | convolution fusion | flops 2147614720 | bytes 19922944 | tf_op jit(solution)/shard_map/dot_general | solution.py:155
  123.1 0.3 subtract_convert_fusion
  123.4 5.9 %convert_reduce_fusion = (f32[128,8]{1,0:T(8,128)S(1)}, bf16[128,8,256]{2,1,0:T(8,128)(2,1)S(1)}) fusion(pred[128,256]{1,0:T(8,128)(4,1)S(1)} %broadcast_compare_fusion, bf16[128,256,256]{2,1,0:T(8,128)(2,1)} %bitcast.57, bf16[128,8,64]{2,1,0:T(8,128)(2,1)S(1)} %get-tuple-element.8, bf16[128,8,64]{2,1,0:T(8,128)(2,1)S(1)} %get-tuple-element.7), kind=kOutput, calls=%fused_computation.36 | convolution fusion | flops 69468416 | bytes 9506816 | tf_op jit(solution)/shard_map/sub | solution.py:186
  129.2 4.6 fusion.31
  133.9 0.3 convolution_convert_fusion.1
  134.2 0.2 reshape.295
  134.5 11.2 %all_to_all.20 = bf16[4,64,1024]{2,1,0:T(8,128)(2,1)S(1)} all-to-all(bf16[4,64,1024]{2,1,0:T(8,128)(2,1)S(1)} %reshape.295), channel_id=1, replica_groups=mesh['group'=4,'tensor'=8] {'group'}, dimensions={0} | all-to-all | bytes 1048576 | tf_op jit(solution)/shard_map/all_to_all | solution.py:117
  145.7 3.5 fusion.11
  149.2 34.2 %psum.15 = bf16[16,16,64]{2,1,0:T(8,128)(2,1)S(1)} all-reduce(f32[16,16,64]{2,1,0:T(8,128)S(1)} %fusion.11), channel_id=1, replica_groups=mesh['group'=4,'tensor'=8] {'tensor'}, use_global_device_ids=true, to_apply=%region_6.7 | all-reduce | flops 16384 | bytes 98304 | tf_op jit(solution)/shard_map/psum | solution.py:46
  183.4 4.5 fusion.9
  187.8 3.7 all-to-all-start.3
  191.6 10.1 %fusion.34 = f32[128,8192]{1,0:T(8,128)} fusion(bf16[1024,8192]{1,0:T(8,128)(2,1)} %param.14, bf16[16,8,8,128]{3,2,1,0:T(8,128)(2,1)S(1)} %bitcast.64), kind=kOutput, calls=%fused_computation.42 | convolution fusion | flops 2147483648 | bytes 21233664 | tf_op jit(solution)/shard_map/dot_general | solution.py:209
  201.6 4.1 all-to-all-done.3
  205.9 0.5 convolution_multiply_fusion
  206.5 1.9 add_dynamic-update-slice_fusion
  208.5 92.2 %collective-permute-done = f32[128,8192]{1,0:T(8,128)S(1)} collective-permute-done((f32[128,8192]{1,0:T(8,128)}, f32[128,8192]{1,0:T(8,128)S(1)}, u32[]{:S(2)}, u32[]{:S(2)}) %collective-permute-start) | collective-permute-done | bytes 4194336 | tf_op jit(solution)/shard_map/ppermute | solution.py:20
  300.7 2.7 add.137
  303.5 91.1 %collective-permute-done.1 = f32[128,8192]{1,0:T(8,128)S(1)} collective-permute-done((f32[128,8192]{1,0:T(8,128)S(1)}, f32[128,8192]{1,0:T(8,128)S(1)}, u32[]{:S(2)}, u32[]{:S(2)}) %collective-permute-start.1) | collective-permute-done | bytes 4194336 | tf_op jit(solution)/shard_map/ppermute | solution.py:20
  394.6 0.5 add.138
  395.2 0.2 collective-permute-start.2
  395.4 181.0 %collective-permute-done.2 = f32[128,8192]{1,0:T(8,128)S(1)} collective-permute-done((f32[128,8192]{1,0:T(8,128)S(1)}, f32[128,8192]{1,0:T(8,128)S(1)}, u32[]{:S(2)}, u32[]{:S(2)}) %collective-permute-start.2) | collective-permute-done | bytes 4194336 | tf_op jit(solution)/shard_map/ppermute | solution.py:20
  576.3 2.0 fusion.8
  (48 shorter events, 1.9 us)
Async XLA Ops:
  0.0 96.6 %copy-start = (bf16[192,1,32,256]{3,2,1,0:T(8,128)(2,1)S(1)}, bf16[192,1,32,256]{3,2,1,0:T(8,128)(2,1)}, u32[]{:S(2)}) copy-start(bf16[192,1,32,256]{3,2,1,0:T(8,128)(2,1)} %param.15) | copy-start | bytes 9437188
  2.2 15.7 %copy-start.7 = (s32[32]{0:T(128)S(1)}, s32[32]{0:T(128)}, u32[]{:S(2)}) copy-start(s32[32]{0:T(128)} %param.21) | copy-start | bytes 388
  2.2 15.9 %copy-start.6 = (s32[1,128]{1,0:T(1,128)S(1)}, s32[1,128]{1,0:T(1,128)}, u32[]{:S(2)}) copy-start(s32[1,128]{1,0:T(1,128)} %param.17) | copy-start | bytes 1540
  5.1 13.4 %copy-start.8 = (s32[1,128]{1,0:T(1,128)S(1)}, s32[1,128]{1,0:T(1,128)}, u32[]{:S(2)}) copy-start(s32[1,128]{1,0:T(1,128)} %param.18) | copy-start | bytes 1540
  5.1 13.7 %copy-start.2 = (s32[1,192]{1,0:T(1,128)S(1)}, s32[1,192]{1,0:T(1,128)}, u32[]{:S(2)}) copy-start(s32[1,192]{1,0:T(1,128)} %param.16) | copy-start | bytes 2308
  7.3 1.3 copy-start.4
  13.7 30.9 %all-to-all-start = ((bf16[4,64,1024]{2,1,0:T(8,128)(2,1)}), bf16[4,64,1024]{2,1,0:T(8,128)(2,1)}, u32[]{:S(2)}, u32[]{:S(2)}) async-start(bf16[4,64,1024]{2,1,0:T(8,128)(2,1)} %reshape.285), calls=%async_computation | async-start | bytes 1048576 | tf_op jit(solution)/shard_map/all_to_all | solution.py:117
  92.2 18.7 %all-to-all-start.1 = ((f32[4,64,1024]{2,1,0:T(8,128)}), f32[4,64,1024]{2,1,0:T(8,128)}, u32[]{:S(2)}, u32[]{:S(2)}) async-start(f32[4,64,1024]{2,1,0:T(8,128)} %bitcast.62), calls=%async_computation.1 | async-start | bytes 2097152 | tf_op jit(solution)/shard_map/all_to_all | solution.py:138
  109.1 5.8 copy-start.5
  187.8 17.9 %all-to-all-start.3 = ((f32[4,64,1024]{2,1,0:T(8,128)}), f32[4,64,1024]{2,1,0:T(8,128)S(1)}, u32[]{:S(2)}, u32[]{:S(2)}) async-start(f32[4,64,1024]{2,1,0:T(8,128)} %bitcast.11), calls=%async_computation.3 | async-start | bytes 2097152 | tf_op jit(solution)/shard_map/all_to_all | solution.py:138
  208.4 92.2 %collective-permute-start = (f32[128,8192]{1,0:T(8,128)}, f32[128,8192]{1,0:T(8,128)S(1)}, u32[]{:S(2)}, u32[]{:S(2)}) collective-permute-start(f32[128,8192]{1,0:T(8,128)} %add_dynamic-update-slice_fusion), channel_id=1, source_target_pairs={{0,1},{1,0},{2,3},{3,2},{4,5},{5,4},{6,7},{7,6},{8,9},{9,8},{10,11... | collective-permute-start | bytes 12582920 | tf_op jit(solution)/shard_map/ppermute | solution.py:20
  303.4 272.9 %copy-start.3 = (bf16[128,8192]{1,0:T(8,128)(2,1)S(1)}, bf16[128,8192]{1,0:T(8,128)(2,1)}, u32[]{:S(2)}) copy-start(bf16[128,8192]{1,0:T(8,128)(2,1)} %param.11) | copy-start | bytes 6291460
  303.4 91.2 %collective-permute-start.1 = (f32[128,8192]{1,0:T(8,128)S(1)}, f32[128,8192]{1,0:T(8,128)S(1)}, u32[]{:S(2)}, u32[]{:S(2)}) collective-permute-start(f32[128,8192]{1,0:T(8,128)S(1)} %add.137), channel_id=1, source_target_pairs={{0,2},{1,3},{2,0},{3,1},{4,6},{5,7},{6,4},{7,5},{8,10},{9,11},{10,... | collective-permute-start | bytes 12582920 | tf_op jit(solution)/shard_map/ppermute | solution.py:20
  394.6 183.7 %copy-start.1 = (bf16[192,1,32,256]{3,2,1,0:T(8,128)(2,1)S(1)}, bf16[192,1,32,256]{3,2,1,0:T(8,128)(2,1)}, u32[]{:S(2)}) copy-start(bf16[192,1,32,256]{3,2,1,0:T(8,128)(2,1)} %param.15) | copy-start | bytes 9437188
  395.2 181.2 %collective-permute-start.2 = (f32[128,8192]{1,0:T(8,128)S(1)}, f32[128,8192]{1,0:T(8,128)S(1)}, u32[]{:S(2)}, u32[]{:S(2)}) collective-permute-start(f32[128,8192]{1,0:T(8,128)S(1)} %add.138), channel_id=1, source_target_pairs={{0,4},{1,5},{2,6},{3,7},{4,0},{5,1},{6,2},{7,3},{8,12},{9,13},{10,... | collective-permute-start | bytes 12582920 | tf_op jit(solution)/shard_map/ppermute | solution.py:20
